TPU v7x, 256 devices: a whole 4x4x8 slice. The times are simulated.
256 devices in a mesh: row: 8 (over z), col: 16 (over x_hi, y, core), rep: 2 (over x_lo).
Axes of the slice: x: 4 (x_hi: 2, x_lo: 2; x = x_hi * 2 + x_lo), y: 4, z: 8, core: 2. Of those that a mesh axis runs over, the one named last changes fastest.
Arguments:
- descriptors: float32 [2048, 256], P('rep', 'col'), may hold values from -6 to 6
- landmarks: float32 [12288, 256], P('row', 'col'), may hold values from -6 to 6
- whitening: float32 [12288, 12288], P('row', 'col'), may hold values from -1 to 1
- assign: int32 [2048], replicated, may hold values from 0 to 4095
Outputs:
- cluster_sums: float32 [4096, 12288], P(('row', 'rep'), 'col')
All inputs are finite; a program needn't handle non-finite values.
Results may differ from a plain program's by a relative error of at most 0.00016.
Values sent between devices are 32-bit elements; how exact they have to be, the bound alone decides.
A program may use at most 64 MiB of HBM per device.

v0:
```python
import jax
import jax.numpy as jnp
from jax import lax
from jax.sharding import PartitionSpec as P

SPREAD = 51
CLUSTERS = 4096
highest = lax.Precision.HIGHEST


def kernel_tile(points, centres):
    row_square = jnp.sum(points * points, axis=1)
    centre_square = jnp.sum(centres * centres, axis=1)
    inner = jnp.dot(points, centres.T, precision=highest, preferred_element_type=jnp.float32)
    distance = row_square[:, None] + centre_square[None, :] - 2.0 * inner
    return jnp.exp(-distance / (2.0 * SPREAD))


def per_device(descriptors, landmarks, whitening, assign):
    part_rows = descriptors.shape[0]
    rep_position = lax.axis_index("rep")
    full_points, full_centres = (
        lax.all_gather(descriptors, "col", axis=1, tiled=True),
        lax.all_gather(landmarks, "col", axis=1, tiled=True),
    )
    kernel = kernel_tile(full_points, full_centres)
    whitened = jnp.dot(kernel, whitening, precision=highest, preferred_element_type=jnp.float32)
    owned_count = CLUSTERS // (lax.axis_size("row") * lax.axis_size("rep"))
    local_assign = lax.dynamic_slice_in_dim(assign, rep_position * part_rows, part_rows)
    labels = jnp.arange(owned_count * lax.axis_size(("row", "rep")), dtype=jnp.int32)
    onehot = (labels[:, None] == local_assign[None, :]).astype(jnp.float32)
    return lax.psum_scatter(
        jnp.dot(onehot, whitened, precision=highest, preferred_element_type=jnp.float32),
        ("row", "rep"),
        scatter_dimension=0,
        tiled=True,
    )


def solution(mesh):
    placed = (P("rep", "col"), P("row", "col"), P("row", "col"), P())
    return jax.shard_map(
        per_device, mesh=mesh, in_specs=placed, out_specs=P(("row", "rep"), "col"), check_vma=False
    )
```

profile of v0, /device:TPU:1, one launch (start us, length us, event | category | flops | bytes accessed | tf_op | source)
XLA Modules:
  0.0 440.5 jit_solution(17535972358049037863)
XLA Ops:
  6.5 0.0 all-gather.3.cloned.1.call-start
  6.5 0.7 all-gather.3.cloned.1.call-update
  7.3 0.0 all-gather.5.cloned.1.call-start
  7.3 0.7 all-gather.5.cloned.1.call-update
  8.0 0.0 reduce-scatter.2.cloned.1.call-start
  8.1 56.2 %all-gather.3.cloned.1.call-done = f32[1024,256]{0,1:T(8,128)} async-done(((f32[1024,16]{0,1:T(8,128)}), f32[1024,256]{0,1:T(8,128)}) %all-gather.3.cloned.1.call-update) | async-done | bytes 1048592 | tf_op jit(solution)/shard_map/all_gather | solution.py:23
  64.2 1.3 multiply_reduce_fusion.1
  65.6 51.5 %all-gather.5.cloned.1.call-done = f32[1536,256]{0,1:T(8,128)} async-done(((f32[1536,16]{0,1:T(8,128)}), f32[1536,256]{0,1:T(8,128)}) %all-gather.5.cloned.1.call-update) | async-done | bytes 1572880 | tf_op jit(solution)/shard_map/all_gather | solution.py:24
  117.1 0.0 slice-start
  117.1 1.7 multiply_reduce_fusion
  118.8 0.0 slice-start.1
  118.8 7.3 %fusion.15 = f32[1024,1536]{1,0:T(8,128)S(1)} fusion(f32[1024,256]{0,1:T(8,128)} %all-gather.3.cloned.1.call-done, f32[1536,256]{0,1:T(8,128)} %all-gather.5.cloned.1.call-done), kind=kOutput, calls=%fused_computation.18 | convolution fusion | flops 4831838208 | bytes 8912896 | tf_op jit(solution)/shard_map/dot_general | solution.py:14
  126.1 0.0 slice-done
  126.2 0.0 slice-done.1
  126.2 0.0 dynamic-slice-start
  126.2 16.3 %fusion.2 = f32[1024,768]{1,0:T(8,128)S(1)} fusion(f32[1536,768]{1,0:T(8,128)S(1)} %bitcast.5, f32[1024,1536]{1,0:T(8,128)S(1)} %fusion.15, f32[1536]{0:T(1024)S(1)} %multiply_reduce_fusion, f32[1024]{0:T(1024)S(1)} %multiply_reduce_fusion.1), kind=kOutput, calls=%fused_computation.3 | convolution fusion | flops 14503378944 | bytes 14166016 | tf_op jit(solution)/shard_map/dot_general | solution.py:27
  142.5 0.0 dynamic-slice-done
  142.5 25.8 %fusion = f32[4096,768]{1,0:T(8,128)} fusion(f32[1024,768]{1,0:T(8,128)S(1)} %fusion.2, s32[1024]{0:T(1024)S(1)} %dynamic-slice-done), kind=kOutput, calls=%fused_computation.1 | convolution fusion | flops 38658899968 | bytes 15732736 | tf_op jit(solution)/shard_map/dot_general | solution.py:33
  168.3 0.0 reduce-scatter.2.cloned.1.call-update
  168.3 265.7 %reduce-scatter.2.cloned.1.call-done = f32[256,768]{1,0:T(8,128)} async-done(((f32[4096,768]{1,0:T(8,128)}), f32[256,768]{1,0:T(8,128)}) %reduce-scatter.2.cloned.1.call-update) | async-done | bytes 786448 | tf_op jit(solution)/shard_map/reduce_scatter | solution.py:32
  (1 shorter events, 0.0 us)
Async XLA Ops:
  6.5 57.7 %all-gather.3.cloned.1.call-start = ((), (), s32[]{:S(2)}) async-start(), calls=%async_computation.1 | async-start | bytes 1114112 | tf_op jit(solution)/shard_map/all_gather | solution.py:23
  7.3 109.8 %all-gather.5.cloned.1.call-start = ((), (), s32[]{:S(2)}) async-start(), calls=%async_computation.2 | async-start | bytes 1671168 | tf_op jit(solution)/shard_map/all_gather | solution.py:24
  8.0 426.0 %reduce-scatter.2.cloned.1.call-start = ((), (), s32[]{:S(2)}) async-start(), calls=%async_computation.3 | async-start | bytes 13369344 | tf_op jit(solution)/shard_map/reduce_scatter | solution.py:32
  117.1 9.0 %slice-start = ((s8[4718592]{0:T(1024)(128)(4,1)}), s8[4194304]{0:T(1024)(128)(4,1)S(1)}, s32[]{:S(2)}) async-start(s8[4718592]{0:T(1024)(128)(4,1)} %bitcast.4), calls=%async_computation.5 | async-start | bytes 8388608
  118.8 7.4 %slice-start.1 = ((s8[4718592]{0:T(1024)(128)(4,1)}), s8[524288]{0:T(1024)(128)(4,1)S(1)}, s32[]{:S(2)}) async-start(s8[4718592]{0:T(1024)(128)(4,1)} %bitcast.4), calls=%async_computation.6 | async-start | bytes 1048576
  126.2 16.3 %dynamic-slice-start = ((s32[2048]{0:T(1024)}, s32[]{:T(128)}), s32[1024]{0:T(1024)S(1)}, s32[]{:S(2)}) async-start(s32[2048]{0:T(1024)} %param.7, s32[]{:T(128)} %select_n.3), calls=%async_computation.4 | async-start | bytes 8704 | tf_op jit(solution)/shard_map/dynamic_slice | solution.py:29
Sparse Core Ops, SparseCore 0:
  10.1 54.0 all-gather.2
  67.0 50.0 all-gather.4
  168.4 265.5 reduce-scatter.1
where the time goes:
time: 441 us
  waiting for transfers between devices  375 us (85%)
  matrix products  49.4 us (11%)
  between operations  13.2 us (3%)
    reduce_scatter x1, waiting for transfers between devices, per_device(): lax.psum_scatter(jnp.dot(onehot, whitened, precision=highest, preferred_e...  266 us
    all_gather x1, waiting for transfers between devices, per_device(): lax.all_gather(descriptors, 'col', axis=1, tiled=True)  56.2 us
    all_gather x1, waiting for transfers between devices, per_device(): lax.all_gather(landmarks, 'col', axis=1, tiled=True)  51.5 us
    dot_general x1, matrix products, per_device(): jnp.dot(onehot, whitened, precision=highest, preferred_element_type=jnp.f...  25.8 us
    dot_general x1, matrix products, per_device(): jnp.dot(kernel, whitening, precision=highest, preferred_element_type=jnp....  16.3 us
  transfers between devices with their start and end apart: 3, of which 3 were waited for; matrix products, arithmetic and copies ran while one was open for 0% of the time, Pallas kernels for 0%

commit v1 on v0

--- a/solution.py
+++ b/solution.py
@@ -20,7 +20,9 @@
     part_rows = descriptors.shape[0]
     rep_position = lax.axis_index("rep")
     full_points, full_centres = (
-        lax.all_gather(descriptors, "col", axis=1, tiled=True),
+        jnp.concatenate(
+            lax.all_to_all(jnp.stack([descriptors] * lax.axis_size("col")), "col", 0, 0), axis=1
+        ),
         lax.all_gather(landmarks, "col", axis=1, tiled=True),
     )
     kernel = kernel_tile(full_points, full_centres)

time: 441 us -> 391 us (0.89)
  waiting for transfers between devices: 375 us -> 316 us
  starting transfers between devices: 0.08 us -> 8.49 us
    all_gather x1 -> x0, waiting for transfers between devices: 56.2 us -> none  [per_device(): lax.all_gather(descriptors, 'col', axis=1, tiled=True)]
    all_gather x1, waiting for transfers between devices: 51.5 us -> 31.5 us  [per_device(): lax.all_gather(landmarks, 'col', axis=1, tiled=True)]
    all_to_all x0 -> x1, waiting for transfers between devices: none -> 18.2 us  [per_device(): lax.all_to_all(jnp.stack([descriptors] * lax.axis_size('col')), 'col', 0, 0)]
    all_to_all x0 -> x1, starting transfers between devices: none -> 8.45 us  [per_device(): lax.all_to_all(jnp.stack([descriptors] * lax.axis_size('col')), 'col', 0, 0)]
  transfers between devices with their start and end apart: 3 -> 3, of which waited for: 3 -> 3; matrix products, arithmetic and copies ran while one was open for 0% -> 1% of each run, Pallas kernels for 0% -> 0%
where the time goes in v1:
time: 391 us
  waiting for transfers between devices  316 us (81%)
  matrix products  49.1 us (13%)
  between operations  13.5 us (3%)
  starting transfers between devices  8.49 us (2%)
    reduce_scatter x1, waiting for transfers between devices, per_device(): lax.psum_scatter(jnp.dot(onehot, whitened, precision=highest, preferred_e...  266 us
    all_gather x1, waiting for transfers between devices, per_device(): lax.all_gather(landmarks, 'col', axis=1, tiled=True)  31.5 us
    dot_general x1, matrix products, per_device(): jnp.dot(onehot, whitened, precision=highest, preferred_element_type=jnp.f...  25.7 us
    all_to_all x1, waiting for transfers between devices, per_device(): lax.all_to_all(jnp.stack([descriptors] * lax.axis_size('col')), 'col', 0, 0)  18.2 us
    dot_general x1, matrix products, per_device(): jnp.dot(kernel, whitening, precision=highest, preferred_element_type=jnp....  16.3 us
    all_to_all x1, starting transfers between devices, per_device(): lax.all_to_all(jnp.stack([descriptors] * lax.axis_size('col')), 'col', 0, 0)  8.45 us
  transfers between devices with their start and end apart: 3, of which 3 were waited for; matrix products, arithmetic and copies ran while one was open for 1% of the time, Pallas kernels for 0%

profile of v1, /device:TPU:1, one launch (start us, length us, event | category | flops | bytes accessed | tf_op | source)
XLA Modules:
  0.0 390.9 jit_solution(14331177284963219820)
XLA Ops:
  6.5 0.0 all-gather.2.cloned.1.call-start
  6.5 0.7 all-gather.2.cloned.1.call-update
  7.3 1.9 stack.2
  9.2 8.4 %all-to-all-start = ((f32[16,1024,16]{1,2,0:T(8,128)}), f32[16,1024,16]{1,2,0:T(8,128)S(1)}, u32[]{:S(2)}, u32[]{:S(2)}) async-start(f32[16,1024,16]{1,2,0:T(8,128)} %stack.2), calls=%async_computation | async-start | bytes 2097152 | tf_op jit(solution)/shard_map/all_to_all | solution.py:24
  17.6 0.0 reduce-scatter.2.cloned.1.call-start
  17.7 18.2 %all-to-all-done = f32[16,1024,16]{1,2,0:T(8,128)S(1)} async-done(((f32[16,1024,16]{1,2,0:T(8,128)}), f32[16,1024,16]{1,2,0:T(8,128)S(1)}, u32[]{:S(2)}, u32[]{:S(2)}) %all-to-all-start) | async-done | bytes 1048608 | tf_op jit(solution)/shard_map/all_to_all | solution.py:24
  35.9 0.1 fusion.13
  36.0 31.5 %all-gather.2.cloned.1.call-done = f32[1536,256]{0,1:T(8,128)} async-done(((f32[1536,16]{0,1:T(8,128)}), f32[1536,256]{0,1:T(8,128)}) %all-gather.2.cloned.1.call-update) | async-done | bytes 1572880 | tf_op jit(solution)/shard_map/all_gather | solution.py:26
  67.5 0.0 slice-start
  67.5 1.7 multiply_reduce_fusion
  69.2 0.0 slice-start.1
  69.2 7.0 %fusion.16 = f32[1024,1536]{1,0:T(8,128)S(1)} fusion(f32[1024,256]{0,1:T(8,128)S(1)} %bitcast.10, f32[1536,256]{0,1:T(8,128)} %all-gather.2.cloned.1.call-done), kind=kOutput, calls=%fused_computation.19 | convolution fusion | flops 4831838208 | bytes 8912896 | tf_op jit(solution)/shard_map/dot_general | solution.py:14
  76.2 0.0 slice-done
  76.2 0.0 slice-done.1
  76.2 0.0 dynamic-slice-start
  76.2 16.3 %fusion.2 = f32[1024,768]{1,0:T(8,128)S(1)} fusion(f32[1536,768]{1,0:T(8,128)S(1)} %bitcast.12, f32[1024,1536]{1,0:T(8,128)S(1)} %fusion.16, f32[1536]{0:T(1024)S(1)} %multiply_reduce_fusion, f32[1024]{0:T(1024)S(1)} %fusion.13), kind=kOutput, calls=%fused_computation.3 | convolution fusion | flops 14503378944 | bytes 14166016 | tf_op jit(solution)/shard_map/dot_general | solution.py:29
  92.6 0.0 dynamic-slice-done
  92.6 25.7 %fusion = f32[4096,768]{1,0:T(8,128)} fusion(f32[1024,768]{1,0:T(8,128)S(1)} %fusion.2, s32[1024]{0:T(1024)S(1)} %dynamic-slice-done), kind=kOutput, calls=%fused_computation.1 | convolution fusion | flops 38658899968 | bytes 15732736 | tf_op jit(solution)/shard_map/dot_general | solution.py:35
  118.3 0.0 reduce-scatter.2.cloned.1.call-update
  118.3 265.7 %reduce-scatter.2.cloned.1.call-done = f32[256,768]{1,0:T(8,128)} async-done(((f32[4096,768]{1,0:T(8,128)}), f32[256,768]{1,0:T(8,128)}) %reduce-scatter.2.cloned.1.call-update) | async-done | bytes 786448 | tf_op jit(solution)/shard_map/reduce_scatter | solution.py:34
  (1 shorter events, 0.0 us)
Async XLA Ops:
  6.5 61.0 %all-gather.2.cloned.1.call-start = ((), (), s32[]{:S(2)}) async-start(), calls=%async_computation.2 | async-start | bytes 1671168 | tf_op jit(solution)/shard_map/all_gather | solution.py:26
  9.2 26.7 %all-to-all-start = ((f32[16,1024,16]{1,2,0:T(8,128)}), f32[16,1024,16]{1,2,0:T(8,128)S(1)}, u32[]{:S(2)}, u32[]{:S(2)}) async-start(f32[16,1024,16]{1,2,0:T(8,128)} %stack.2), calls=%async_computation | async-start | bytes 2097152 | tf_op jit(solution)/shard_map/all_to_all | solution.py:24
  17.6 366.4 %reduce-scatter.2.cloned.1.call-start = ((), (), s32[]{:S(2)}) async-start(), calls=%async_computation.3 | async-start | bytes 13369344 | tf_op jit(solution)/shard_map/reduce_scatter | solution.py:34
  67.5 8.7 %slice-start = ((s8[4718592]{0:T(1024)(128)(4,1)}), s8[4194304]{0:T(1024)(128)(4,1)S(1)}, s32[]{:S(2)}) async-start(s8[4718592]{0:T(1024)(128)(4,1)} %bitcast.11), calls=%async_computation.5 | async-start | bytes 8388608
  69.2 7.0 %slice-start.1 = ((s8[4718592]{0:T(1024)(128)(4,1)}), s8[524288]{0:T(1024)(128)(4,1)S(1)}, s32[]{:S(2)}) async-start(s8[4718592]{0:T(1024)(128)(4,1)} %bitcast.11), calls=%async_computation.6 | async-start | bytes 1048576
  76.2 16.3 %dynamic-slice-start = ((s32[2048]{0:T(1024)}, s32[]{:T(128)}), s32[1024]{0:T(1024)S(1)}, s32[]{:S(2)}) async-start(s32[2048]{0:T(1024)} %param.7, s32[]{:T(128)} %select_n.3), calls=%async_computation.4 | async-start | bytes 8704 | tf_op jit(solution)/shard_map/dynamic_slice | solution.py:31
Sparse Core Ops, SparseCore 0:
  10.1 57.3 all-gather.1
  118.5 265.5 reduce-scatter.1
